TPU v7x, 32 devices: a whole 2x2x4 slice. The times are simulated.
32 devices in a mesh: dp: 16 (over z, y, x), mp: 2 (over core).
Axes of the slice: x: 2, y: 2, z: 4, core: 2. Of those that a mesh axis runs over, the one named last changes fastest.
Arguments:
- gradient: bfloat16 [2, 8, 512, 512], P('mp', None, 'dp'), may hold values from -54 to 54
- owners: int32 [2, 8], P('mp'), may hold values from 0 to 15, as said below
- left_stats: float32 [2, 16, 512, 512], P('mp', 'dp'), may hold values from -0.2 to 20.2
- right_stats: float32 [2, 16, 512, 512], P('mp', 'dp'), may hold values from -0.2 to 20.2
- left_roots_old: bfloat16 [2, 16, 512, 512], P('mp', 'dp'), may hold values from -0.1 to 1.5
- right_roots_old: bfloat16 [2, 16, 512, 512], P('mp', 'dp'), may hold values from -0.1 to 1.5
Outputs:
- update: bfloat16 [2, 8, 512, 512], P('mp', None, 'dp')
- left_roots: bfloat16 [2, 16, 512, 512], P('mp', 'dp')
- right_roots: bfloat16 [2, 16, 512, 512], P('mp', 'dp')
Inputs may be any that keep to these rules, and one draw needn't show every extreme that they name: In each row the 8 owners are distinct. Owner o holds a block of row m exactly when owner (o + 8) mod 16 of row m holds none, and exactly when owner o of row (m + 1) mod 2 holds none.
All inputs are finite; a program needn't handle non-finite values.
Results may differ from a plain program's by a relative error of at most 0.0067.
Values may be sent and summed in bfloat16 or wider, within the bound.
A program may use at most 64 MiB of HBM per device.

v0:
```python
import jax
import jax.numpy as jnp
from jax import lax
from jax.sharding import PartitionSpec as P

ITERS = 2
stat_decay = 0.9
ridge_term = 0.001
tiny_term = 1e-06


def newton_root(statistic):
    dimension = statistic.shape[0]
    identity = jnp.eye(dimension, dtype=jnp.float32)
    shifted = statistic + ridge_term * identity
    norm_scale = jnp.sqrt(jnp.sum(shifted * shifted) + tiny_term)
    matrix = shifted / norm_scale
    iterate = identity
    for iteration in range(ITERS):
        factor = ((5.0 * identity - matrix) / 4.0).astype(jnp.bfloat16)
        if iteration == 0:
            iterate = norm_scale ** (-0.25) * lax.optimization_barrier(factor).astype(jnp.float32)
        else:
            iterate = jnp.dot(
                iterate.astype(jnp.bfloat16), factor, preferred_element_type=jnp.float32
            )
        if iteration + 1 < ITERS:
            factor_two = jnp.dot(factor, factor, preferred_element_type=jnp.float32).astype(
                jnp.bfloat16
            )
            factor_four = jnp.dot(
                factor_two, factor_two, preferred_element_type=jnp.float32
            ).astype(jnp.bfloat16)
            matrix = jnp.dot(
                factor_four, matrix.astype(jnp.bfloat16), preferred_element_type=jnp.float32
            )
    return iterate.astype(jnp.bfloat16)


def shards(gradient, owners, left_stats, right_stats, left_roots_old, right_roots_old):
    dp_count = lax.axis_size("dp")
    my_index = lax.axis_index("dp")
    blocks_here = gradient.shape[1]
    row_count = gradient.shape[2]
    block_width = gradient.shape[3]
    owner_table = owners[0]
    owner_ids = jnp.arange(dp_count, dtype=jnp.int32)
    selector = (owner_table[None, :] == owner_ids[:, None]).astype(jnp.bfloat16)
    flat_grad = gradient[0].reshape(blocks_here, row_count * block_width)
    outgoing = jnp.dot(selector, flat_grad, preferred_element_type=jnp.float32).astype(jnp.bfloat16)
    outgoing = outgoing.reshape(dp_count, row_count, block_width)
    arrived = lax.all_to_all(outgoing, "dp", split_axis=0, concat_axis=1, tiled=True)
    grad_block = arrived[0]
    is_mine = owner_table == my_index
    mine_weight = is_mine.astype(jnp.float32)
    is_busy = jnp.any(is_mine)
    left_gram = jnp.einsum("ik,jk->ij", grad_block, grad_block, preferred_element_type=jnp.float32)
    right_gram = jnp.einsum("ki,kj->ij", grad_block, grad_block, preferred_element_type=jnp.float32)
    left_new = stat_decay * left_stats[0, 0] + left_gram / block_width
    right_new = stat_decay * right_stats[0, 0] + right_gram / block_width
    shaded = jnp.dot(grad_block, right_roots_old[0, 0], preferred_element_type=jnp.float32).astype(
        jnp.bfloat16
    )
    direction = jnp.dot(left_roots_old[0, 0], shaded, preferred_element_type=jnp.float32).astype(
        jnp.bfloat16
    )
    squares = jnp.stack(
        [
            jnp.sum(jnp.square(grad_block.astype(jnp.float32))),
            jnp.sum(jnp.square(direction.astype(jnp.float32))),
        ]
    )
    graft_terms = squares[:, None] * mine_weight[None, :]
    returned = lax.all_to_all(direction[None], "dp", split_axis=1, concat_axis=0, tiled=True)
    totals = lax.psum(graft_terms, ("dp", "mp"))
    graft_scale = jnp.sqrt(totals[0] / (totals[1] + tiny_term))
    pieces = jnp.einsum(
        "on,or->nr",
        selector,
        returned.reshape(dp_count, row_count * block_width),
        preferred_element_type=jnp.float32,
    )
    update = (
        (graft_scale[:, None] * pieces)
        .astype(jnp.bfloat16)
        .reshape(1, blocks_here, row_count, block_width)
    )
    zero_root = jnp.zeros((block_width, block_width), jnp.bfloat16)
    left_root, right_root = lax.cond(
        is_busy,
        lambda: (newton_root(left_new), newton_root(right_new)),
        lambda: (zero_root, zero_root),
    )
    return (update, left_root[None, None], right_root[None, None])


def solution(mesh):
    return jax.shard_map(
        shards,
        mesh=mesh,
        in_specs=(
            P("mp", None, "dp", None),
            P("mp", None),
            P("mp", "dp", None, None),
            P("mp", "dp", None, None),
            P("mp", "dp", None, None),
            P("mp", "dp", None, None),
        ),
        out_specs=(P("mp", None, "dp", None), P("mp", "dp", None, None), P("mp", "dp", None, None)),
        check_vma=False,
    )
```

profile of v0, /device:TPU:0, one launch (start us, length us, event | category | flops | bytes accessed | tf_op | source)
XLA Modules:
  0.0 111.4 jit_solution(4444039082128814350)
XLA Ops:
  0.6 1.2 %copy.18 = bf16[1,8,32,512]{3,1,2,0:T(8,128)(2,1)S(1)} copy(bf16[1,8,32,512]{3,2,1,0:T(8,128)(2,1)} %param.8) | data formatting | bytes 524288
  1.8 0.6 copy-done.4
  2.5 0.3 convolution_convert_fusion.6
  2.7 1.0 copy.19
  3.7 8.5 %all-to-all-start = ((bf16[16,32,512]{2,1,0:T(8,128)(2,1)}), bf16[16,32,512]{2,1,0:T(8,128)(2,1)S(1)}, u32[]{:S(2)}, u32[]{:S(2)}) async-start(bf16[16,32,512]{2,1,0:T(8,128)(2,1)} %bitcast.21), calls=%async_computation | async-start | bytes 1048576 | tf_op jit(solution)/shard_map/all_to_all | solution.py:52
  12.2 0.6 compare_reduce_fusion
  12.8 14.4 %all-to-all-done = bf16[16,32,512]{2,1,0:T(8,128)(2,1)S(1)} async-done(((bf16[16,32,512]{2,1,0:T(8,128)(2,1)}), bf16[16,32,512]{2,1,0:T(8,128)(2,1)S(1)}, u32[]{:S(2)}, u32[]{:S(2)}) %all-to-all-start) | async-done | bytes 524320 | tf_op jit(solution)/shard_map/all_to_all | solution.py:52
  27.3 1.5 %multiply_reduce_fusion.2 = (f32[]{:T(128)}, bf16[512,512]{1,0:T(8,128)(2,1)S(1)}) fusion(bf16[1,1,512,512]{3,2,1,0:T(8,128)(2,1)S(1)} %copy-done, bf16[512,512]{1,0:T(8,128)(2,1)S(1)} %bitcast.76, bf16[1,1,512,512]{3,2,1,0:T(8,128)(2,1)S(1)} %copy-done.5), kind=kOutput, calls=%fused_computation.53 | convolution fusion | flops 538181632 | bytes 2097156 | tf_op jit(solution)/shard_map/dot_general | solution.py:64
  28.8 0.9 copy.16
  29.7 0.5 broadcast.160
  30.2 3.8 %reduce.3 = bf16[512,512]{1,0:T(8,128)(2,1)S(1)} reduce(bf16[512,1,512]{2,1,0:T(2,128)(2,1)S(1)} %bitcast.78, bf16[]{:T(256)} %broadcast.160), dimensions={1}, to_apply=%bitcast.56.reduce_sub_computation | reduce | bytes 1048578
  34.0 1.2 %reshape.49 = bf16[16,2,8192]{2,1,0:T(2,128)(2,1)} reshape(bf16[512,512]{1,0:T(8,128)(2,1)S(1)} %reduce.3) | data formatting | bytes 1048576
  35.2 4.2 %all-to-all-start.1 = ((bf16[16,2,8192]{2,1,0:T(2,128)(2,1)}), bf16[16,2,8192]{2,1,0:T(2,128)(2,1)}, u32[]{:S(2)}, u32[]{:S(2)}) async-start(bf16[16,2,8192]{2,1,0:T(2,128)(2,1)} %reshape.49), calls=%async_computation.1 | async-start | bytes 1048576 | tf_op jit(solution)/shard_map/all_to_all | solution.py:74
  39.5 0.9 multiply_reduce_fusion.3
  40.3 1.4 %pad_maximum_fusion = f32[2]{0:T(128)S(1)} fusion(f32[1]{0:T(128)} %bitcast.6, f32[1]{0:T(128)} %bitcast.1), kind=kLoop, calls=%fused_computation.63 | loop fusion | flops 2 | bytes 16 | tf_op jit(solution)/shard_map/stack | solution.py:67
  42.4 40.7 %psum.7 = f32[2,8]{1,0:T(2,128)S(1)} all-reduce(f32[2,8]{1,0:T(2,128)S(1)} %broadcast_multiply_fusion), channel_id=1, replica_groups=mesh['dp'=16,'mp'=2] {'dp','mp'}, use_global_device_ids=true, to_apply=%region_2.0 | all-reduce | flops 16 | bytes 128 | tf_op jit(solution)/shard_map/psum | solution.py:75
  83.1 0.5 fusion.37
  83.6 1.5 %convolution_bitcast_fusion = f32[512,512]{1,0:T(8,128)} fusion(bf16[16,32,512]{2,1,0:T(8,128)(2,1)S(1)} %all-to-all-done), kind=kOutput, calls=%fused_computation.50 | convolution fusion | flops 268435456 | bytes 1572864 | tf_op jit(solution)/shard_map/ki,kj->ij/dot_general | solution.py:58
  85.1 18.9 %conditional.1 = (bf16[1,1,512,512]{3,2,1,0:T(8,128)(2,1)S(1)}, bf16[1,1,512,512]{3,2,1,0:T(8,128)(2,1)}) conditional(s32[]{:T(128)} %convert_element_type.101, () %tuple.22, (f32[1,1,512,512]{3,2,1,0:T(8,128)S(1)}, f32[512,512]{1,0:T(8,128)S(1)}, f32[1,1,512,512]{3,2,1,0:T(8,128)}, f32[512,512]{1,0:T(8,128)}) %tuple.39), branch_computations={%region_4.0_spmd, %region_5.0_spmd.clone} | conditional | flops 2166620160 | bytes 20971660 | solution.py:89
  85.1 0.9 multiply_reduce_fusion.1
  86.7 2.4 %multiply_reduce_fusion = f32[]{:T(128)} fusion(f32[512,512]{1,0:T(8,128)} %get-tuple-element.58, f32[1,1,512,512]{3,2,1,0:T(8,128)} %get-tuple-element.60), kind=kLoop, calls=%fused_computation.25 | loop fusion | flops 2097151 | bytes 2097156 | tf_op jit(solution)/shard_map/cond/branch_1_fun/reduce_sum | solution.py:16
  89.8 2.9 %fusion.7 = (bf16[512,512]{1,0:T(8,128)(2,1)S(1)}, bf16[512,512]{1,0:T(8,128)(2,1)}) fusion(f32[]{:T(128)S(6)} %sqrt.20, f32[512,512]{1,0:T(8,128)S(1)} %get-tuple-element.57, f32[1,1,512,512]{3,2,1,0:T(8,128)S(1)} %get-tuple-element.59, f32[]{:T(128)S(6)} %sqrt.21, f32[512,512]{1,0:T(8,128)} %get-tuple-element.58, f32[1,1,512,512]{3,2,1,0:T(8,128)} %get-tuple-element.60), kind=kLoop, calls=%fused_computation.19 | loop fusion | flops 4980736 | bytes 5242888 | tf_op jit(solution)/shard_map/cond/branch_1_fun/convert_element_type | solution.py:20
  92.7 3.6 %convolution_convert_fusion.1 = bf16[512,512]{1,0:T(8,128)(2,1)} fusion(bf16[512,512]{1,0:T(8,128)(2,1)} %get-tuple-element.75), kind=kOutput, calls=%fused_computation.9 | convolution fusion | flops 537395200 | bytes 1048576 | tf_op jit(solution)/shard_map/cond/branch_1_fun/dot_general | solution.py:31
  96.4 3.5 %fusion.5 = bf16[1,1,512,512]{3,2,1,0:T(8,128)(2,1)} fusion(bf16[512,512]{1,0:T(8,128)(2,1)} %convolution_convert_fusion.1, bf16[512,512]{1,0:T(8,128)(2,1)} %get-tuple-element.75, f32[]{:T(128)S(6)} %pow.9, f32[]{:T(128)S(6)} %sqrt.21, f32[1,1,512,512]{3,2,1,0:T(8,128)} %get-tuple-element.60, f32[512,512]{1,0:T(8,128)} %get-tuple-element.58), kind=kOutput, calls=%fused_computation.17 | convolution fusion | flops 541327360 | bytes 3670024 | tf_op jit(solution)/shard_map/cond/branch_1_fun/dot_general | solution.py:24
  99.9 1.8 %convolution_convert_fusion.4 = bf16[512,512]{1,0:T(8,128)(2,1)} fusion(bf16[512,512]{1,0:T(8,128)(2,1)S(1)} %get-tuple-element.74), kind=kOutput, calls=%fused_computation.12 | convolution fusion | flops 537395200 | bytes 1048576 | tf_op jit(solution)/shard_map/cond/branch_1_fun/dot_general | solution.py:31
  101.8 2.1 %fusion.4 = bf16[1,1,512,512]{3,2,1,0:T(8,128)(2,1)S(1)} fusion(bf16[512,512]{1,0:T(8,128)(2,1)} %convolution_convert_fusion.4, bf16[512,512]{1,0:T(8,128)(2,1)} %copy-done.3, f32[]{:T(128)S(6)} %pow.8, f32[]{:T(128)S(6)} %sqrt.20, f32[1,1,512,512]{3,2,1,0:T(8,128)S(1)} %get-tuple-element.59, f32[512,512]{1,0:T(8,128)S(1)} %get-tuple-element.57), kind=kOutput, calls=%fused_computation.16 | convolution fusion | flops 541327360 | bytes 3670024 | tf_op jit(solution)/shard_map/cond/branch_1_fun/dot_general | solution.py:24
  104.0 0.8 copy-done.2
  104.8 2.2 %reshape.50 = bf16[512,1,512]{2,1,0:T(2,128)(2,1)S(1)} reshape(bf16[16,2,8192]{2,1,0:T(2,128)(2,1)} %all-to-all-done.1) | data formatting | bytes 1048576
  107.0 3.1 %bitcast_reduce_fusion = bf16[512,512]{1,0:T(8,128)(2,1)S(1)} fusion(bf16[512,1,512]{2,1,0:T(2,128)(2,1)S(1)} %reshape.50), kind=kLoop, calls=%fused_computation.67 | loop fusion | bytes 1048576 | tf_op jit(solution)/shard_map/all_to_all | solution.py:74
  110.1 0.2 reshape.40
  110.4 0.3 fusion.28
  110.7 0.8 copy.17
  (14 shorter events, 0.1 us)
Async XLA Ops:
  0.6 26.6 %copy-start = (bf16[1,1,512,512]{3,2,1,0:T(8,128)(2,1)S(1)}, bf16[1,1,512,512]{3,2,1,0:T(8,128)(2,1)}, u32[]{:S(2)}) copy-start(bf16[1,1,512,512]{3,2,1,0:T(8,128)(2,1)} %param.12) | copy-start | bytes 1572868
  1.8 0.7 copy-start.4
  3.7 23.6 %copy-start.5 = (bf16[1,1,512,512]{3,2,1,0:T(8,128)(2,1)S(1)}, bf16[1,1,512,512]{3,2,1,0:T(8,128)(2,1)}, u32[]{:S(2)}) copy-start(bf16[1,1,512,512]{3,2,1,0:T(8,128)(2,1)} %param.13) | copy-start | bytes 1572868
  3.7 23.6 %all-to-all-start = ((bf16[16,32,512]{2,1,0:T(8,128)(2,1)}), bf16[16,32,512]{2,1,0:T(8,128)(2,1)S(1)}, u32[]{:S(2)}, u32[]{:S(2)}) async-start(bf16[16,32,512]{2,1,0:T(8,128)(2,1)} %bitcast.21), calls=%async_computation | async-start | bytes 1048576 | tf_op jit(solution)/shard_map/all_to_all | solution.py:52
  35.2 69.6 %all-to-all-start.1 = ((bf16[16,2,8192]{2,1,0:T(2,128)(2,1)}), bf16[16,2,8192]{2,1,0:T(2,128)(2,1)}, u32[]{:S(2)}, u32[]{:S(2)}) async-start(bf16[16,2,8192]{2,1,0:T(2,128)(2,1)} %reshape.49), calls=%async_computation.1 | async-start | bytes 1048576 | tf_op jit(solution)/shard_map/all_to_all | solution.py:74
  83.6 1.5 %copy-start.1 = (f32[1,1,512,512]{3,2,1,0:T(8,128)S(1)}, f32[1,1,512,512]{3,2,1,0:T(8,128)}, u32[]{:S(2)}) copy-start(f32[1,1,512,512]{3,2,1,0:T(8,128)} %param.10) | copy-start | bytes 3145732
  92.7 7.2 %copy-start.3 = (bf16[512,512]{1,0:T(8,128)(2,1)}, bf16[512,512]{1,0:T(8,128)(2,1)S(1)}, u32[]{:S(2)}) copy-start(bf16[512,512]{1,0:T(8,128)(2,1)S(1)} %get-tuple-element.74) | copy-start | bytes 1572868 | tf_op jit(solution)/shard_map/cond
  104.0 0.8 copy-start.2
where the time goes:
time: 112 us; the launch traced here: 111 us
  blocking collectives  40.7 us (36%)
  matrix products  15 us (13%)
  waiting for transfers between devices  14.4 us (13%)
  other arithmetic  13 us (12%)
  starting transfers between devices  12.7 us (11%)
  local copies, waits for them, and re-layouts  12.5 us (11%)
  loops' own time  1.68 us (2%)
  between operations  1.41 us (1%)
    psum x1, blocking collectives, shards(): totals = lax.psum(graft_terms, ('dp', 'mp'))  40.7 us
    all_to_all x1, waiting for transfers between devices, shards(): lax.all_to_all(outgoing, 'dp', split_axis=0, concat_axis=1, tiled=True)  14.4 us
    all_to_all x1, starting transfers between devices, shards(): lax.all_to_all(outgoing, 'dp', split_axis=0, concat_axis=1, tiled=True)  8.47 us
    unnamed x16, local copies, waits for them, and re-layouts  8.25 us
    dot_general x2, matrix products, newton_root(): jnp.dot(iterate.astype(jnp.bfloat16), factor, preferred_element_type=jnp....  5.58 us
    dot_general x2, matrix products, newton_root(): jnp.dot(factor_two, factor_two, preferred_element_type=jnp.float32)  5.42 us
    all_to_all x1, starting transfers between devices, shards(): lax.all_to_all(direction[None], 'dp', split_axis=1, concat_axis=0, tiled=...  4.23 us
    unnamed x1, other arithmetic  3.82 us
  transfers between devices with their start and end apart: 2, of which 1 were waited for; matrix products, arithmetic and copies ran while one was open for 20% of the time, Pallas kernels for 0%

commit v1 on v0

--- a/solution.py
+++ b/solution.py
@@ -49,7 +49,15 @@
     flat_grad = gradient[0].reshape(blocks_here, row_count * block_width)
     outgoing = jnp.dot(selector, flat_grad, preferred_element_type=jnp.float32).astype(jnp.bfloat16)
     outgoing = outgoing.reshape(dp_count, row_count, block_width)
-    arrived = lax.all_to_all(outgoing, "dp", split_axis=0, concat_axis=1, tiled=True)
+    arrived = jnp.concatenate(
+        lax.all_to_all(
+            jnp.stack(jnp.split(outgoing, lax.axis_size("dp"), 0)),
+            axis_name="dp",
+            split_axis=0,
+            concat_axis=0,
+        ),
+        1,
+    )
     grad_block = arrived[0]
     is_mine = owner_table == my_index
     mine_weight = is_mine.astype(jnp.float32)

time: 112 us -> 123 us (1.098)
  local copies, waits for them, and re-layouts: 12.5 us -> 23.9 us
    unnamed x16 -> x28, local copies, waits for them, and re-layouts: 8.25 us -> 15.8 us
    split x0 -> x1, local copies, waits for them, and re-layouts: none -> 2.8 us  [shards(): jnp.split(outgoing, lax.axis_size('dp'), 0)]
  transfers between devices with their start and end apart: 2 -> 2, of which waited for: 1 -> 1; matrix products, arithmetic and copies ran while one was open for 20% -> 18% of each run, Pallas kernels for 0% -> 0%
where the time goes in v1:
time: 123 us
  blocking collectives  40.7 us (33%)
  local copies, waits for them, and re-layouts  23.9 us (19%)
  matrix products  14.8 us (12%)
  waiting for transfers between devices  14.4 us (12%)
  other arithmetic  13.1 us (11%)
  starting transfers between devices  12.7 us (10%)
  loops' own time  1.53 us (1%)
  between operations  1.52 us (1%)
    psum x1, blocking collectives, shards(): totals = lax.psum(graft_terms, ('dp', 'mp'))  40.7 us
    unnamed x28, local copies, waits for them, and re-layouts  15.8 us
    all_to_all x1, waiting for transfers between devices, shards(): lax.all_to_all(jnp.stack(jnp.split(outgoing, lax.axis_size('dp'), 0)), ax...  14.4 us
    all_to_all x1, starting transfers between devices, shards(): lax.all_to_all(jnp.stack(jnp.split(outgoing, lax.axis_size('dp'), 0)), ax...  8.47 us
    dot_general x2, matrix products, newton_root(): jnp.dot(factor_two, factor_two, preferred_element_type=jnp.float32)  5.44 us
    dot_general x2, matrix products, newton_root(): jnp.dot(iterate.astype(jnp.bfloat16), factor, preferred_element_type=jnp....  5.39 us
    all_to_all x1, starting transfers between devices, shards(): lax.all_to_all(direction[None], 'dp', split_axis=1, concat_axis=0, tiled=...  4.23 us
    unnamed x1, other arithmetic  3.95 us
  transfers between devices with their start and end apart: 2, of which 1 were waited for; matrix products, arithmetic and copies ran while one was open for 18% of the time, Pallas kernels for 0%

profile of v1, /device:TPU:0, one launch (start us, length us, event | category | flops | bytes accessed | tf_op | source)
XLA Modules:
  0.0 122.8 jit_solution(4613704231016658092)
XLA Ops:
  0.6 1.2 copy.50
  1.8 0.6 copy-done.5
  2.7 2.8 %slice_reduce_fusion = (bf16[16384]{0:T(1024)(128)(2,1)S(1)}, bf16[16384]{0:T(1024)(128)(2,1)S(1)}, bf16[16384]{0:T(1024)(128)(2,1)S(1)}, bf16[16384]{0:T(1024)(...) fusion(bf16[16,16384]{1,0:T(8,128)(2,1)S(1)} %convolution_conve, ...), kind=kLoop, calls=%fused_computation.58 | loop fusion | bytes 1048576 | tf_op jit(solution)/shard_map/split | solution.py:54
  5.6 0.6 constant_dynamic-update-slice_fusion.15
  6.8 0.6 constant_dynamic-update-slice_fusion.14
  7.4 0.6 constant_dynamic-update-slice_fusion.13
  8.0 0.6 constant_dynamic-update-slice_fusion.12
  8.7 0.6 constant_dynamic-update-slice_fusion.11
  12.4 0.6 constant_dynamic-update-slice_fusion.5
  16.1 8.5 %all-to-all-start = ((bf16[16,1,32,512]{3,2,1,0:T(8,128)(2,1)}), bf16[16,1,32,512]{3,2,1,0:T(8,128)(2,1)S(1)}, u32[]{:S(2)}, u32[]{:S(2)}) async-start(bf16[16,1,32,512]{3,2,1,0:T(8,128)(2,1)} %constant_dynamic-update-slice_fusion), calls=%async_computation | async-start | bytes 1048576 | tf_op jit(solution)/shard_map/all_to_all | solution.py:53
  24.6 0.6 compare_reduce_fusion
  25.2 14.4 %all-to-all-done = bf16[16,1,32,512]{3,2,1,0:T(8,128)(2,1)S(1)} async-done(((bf16[16,1,32,512]{3,2,1,0:T(8,128)(2,1)}), bf16[16,1,32,512]{3,2,1,0:T(8,128)(2,1)S(1)}, u32[]{:S(2)}, u32[]{:S(2)}) %all-to-all-start) | async-done | bytes 524320 | tf_op jit(solution)/shard_map/all_to_all | solution.py:53
  39.6 1.5 %multiply_reduce_fusion.2 = (f32[]{:T(128)}, bf16[512,512]{1,0:T(8,128)(2,1)S(1)}) fusion(bf16[1,1,512,512]{3,2,1,0:T(8,128)(2,1)S(1)} %copy-done, bf16[512,512]{1,0:T(8,128)(2,1)S(1)} %bitcast.75, bf16[1,1,512,512]{3,2,1,0:T(8,128)(2,1)S(1)} %copy-done.6), kind=kOutput, calls=%fused_computation.53 | convolution fusion | flops 538181632 | bytes 2097156 | tf_op jit(solution)/shard_map/dot_general | solution.py:72
  41.2 0.9 copy.48
  42.6 4.0 %reduce.35 = bf16[512,512]{1,0:T(8,128)(2,1)S(1)} reduce(bf16[512,1,512]{2,1,0:T(2,128)(2,1)S(1)} %bitcast.77, bf16[]{:T(256)} %broadcast.176), dimensions={1}, to_apply=%bitcast.57.reduce_sub_computation | reduce | bytes 1048578
  46.5 1.2 reshape.95
  47.7 4.2 %all-to-all-start.1 = ((bf16[16,2,8192]{2,1,0:T(2,128)(2,1)}), bf16[16,2,8192]{2,1,0:T(2,128)(2,1)}, u32[]{:S(2)}, u32[]{:S(2)}) async-start(bf16[16,2,8192]{2,1,0:T(2,128)(2,1)} %reshape.95), calls=%async_computation.1 | async-start | bytes 1048576 | tf_op jit(solution)/shard_map/all_to_all | solution.py:82
  52.0 0.9 multiply_reduce_fusion.3
  52.8 1.4 %pad_maximum_fusion = f32[2]{0:T(128)S(1)} fusion(f32[1]{0:T(128)} %bitcast.6, f32[1]{0:T(128)} %bitcast.1), kind=kLoop, calls=%fused_computation.96 | loop fusion | flops 2 | bytes 16 | tf_op jit(solution)/shard_map/stack | solution.py:75
  54.9 40.7 %psum.7 = f32[2,8]{1,0:T(2,128)S(1)} all-reduce(f32[2,8]{1,0:T(2,128)S(1)} %broadcast_multiply_fusion), channel_id=1, replica_groups=mesh['dp'=16,'mp'=2] {'dp','mp'}, use_global_device_ids=true, to_apply=%region_2.0 | all-reduce | flops 16 | bytes 128 | tf_op jit(solution)/shard_map/psum | solution.py:83
  96.1 1.5 %convolution_bitcast_fusion = f32[512,512]{1,0:T(8,128)} fusion(bf16[16,1,32,512]{3,2,1,0:T(8,128)(2,1)S(1)} %all-to-all-done), kind=kOutput, calls=%fused_computation.50 | convolution fusion | flops 268435456 | bytes 1572864 | tf_op jit(solution)/shard_map/ki,kj->ij/dot_general | solution.py:66
  97.6 18.6 %conditional.1 = (bf16[1,1,512,512]{3,2,1,0:T(8,128)(2,1)}, bf16[1,1,512,512]{3,2,1,0:T(8,128)(2,1)}) conditional(s32[]{:T(128)} %convert_element_type.101, () %tuple.22, (f32[1,1,512,512]{3,2,1,0:T(8,128)S(1)}, f32[512,512]{1,0:T(8,128)S(1)}, f32[1,1,512,512]{3,2,1,0:T(8,128)}, f32[512,512]{1,0:T(8,128)}) %tuple.54), branch_computations={%region_4.0_spmd, %region_5.0_spmd.clone} | conditional | flops 2166620160 | bytes 29360324 | solution.py:97
  97.6 0.9 multiply_reduce_fusion.1
  99.2 2.4 %multiply_reduce_fusion = f32[]{:T(128)} fusion(f32[512,512]{1,0:T(8,128)} %get-tuple-element.58, f32[1,1,512,512]{3,2,1,0:T(8,128)} %get-tuple-element.60), kind=kLoop, calls=%fused_computation.25 | loop fusion | flops 2097151 | bytes 2097156 | tf_op jit(solution)/shard_map/cond/branch_1_fun/reduce_sum | solution.py:16
  102.3 2.9 %fusion.7 = (bf16[512,512]{1,0:T(8,128)(2,1)S(1)}, bf16[512,512]{1,0:T(8,128)(2,1)}) fusion(f32[]{:T(128)S(6)} %sqrt.20, f32[512,512]{1,0:T(8,128)S(1)} %get-tuple-element.57, f32[1,1,512,512]{3,2,1,0:T(8,128)S(1)} %get-tuple-element.59, f32[]{:T(128)S(6)} %sqrt.21, f32[512,512]{1,0:T(8,128)} %get-tuple-element.58, f32[1,1,512,512]{3,2,1,0:T(8,128)} %get-tuple-element.60), kind=kLoop, calls=%fused_computation.19 | loop fusion | flops 4980736 | bytes 5242888 | tf_op jit(solution)/shard_map/cond/branch_1_fun/convert_element_type | solution.py:20
  105.1 1.9 %convolution_convert_fusion.4 = bf16[512,512]{1,0:T(8,128)(2,1)} fusion(bf16[512,512]{1,0:T(8,128)(2,1)S(1)} %get-tuple-element.90), kind=kOutput, calls=%fused_computation.12 | convolution fusion | flops 537395200 | bytes 1048576 | tf_op jit(solution)/shard_map/cond/branch_1_fun/dot_general | solution.py:31
  107.1 2.7 %fusion.4 = bf16[1,1,512,512]{3,2,1,0:T(8,128)(2,1)} fusion(bf16[512,512]{1,0:T(8,128)(2,1)} %convolution_convert_fusion.4, bf16[512,512]{1,0:T(8,128)(2,1)S(1)} %get-tuple-element.90, f32[]{:T(128)S(6)} %pow.8, f32[]{:T(128)S(6)} %sqrt.20, f32[1,1,512,512]{3,2,1,0:T(8,128)S(1)} %get-tuple-element.59, f32[512,512]{1,0:T(8,128)S(1)} %get-tuple-element.57), kind=kOutput, calls=%fused_computation.16 | convolution fusion | flops 541327360 | bytes 3670024 | tf_op jit(solution)/shard_map/cond/branch_1_fun/dot_general | solution.py:24
  109.8 3.6 %convolution_convert_fusion.1 = bf16[512,512]{1,0:T(8,128)(2,1)} fusion(bf16[512,512]{1,0:T(8,128)(2,1)} %get-tuple-element.91), kind=kOutput, calls=%fused_computation.9 | convolution fusion | flops 537395200 | bytes 1048576 | tf_op jit(solution)/shard_map/cond/branch_1_fun/dot_general | solution.py:31
  113.4 2.7 %fusion.5 = bf16[1,1,512,512]{3,2,1,0:T(8,128)(2,1)} fusion(bf16[512,512]{1,0:T(8,128)(2,1)} %convolution_convert_fusion.1, bf16[512,512]{1,0:T(8,128)(2,1)S(1)} %copy-done.4, f32[]{:T(128)S(6)} %pow.9, f32[]{:T(128)S(6)} %sqrt.21, f32[1,1,512,512]{3,2,1,0:T(8,128)S(1)} %copy-done.2, f32[512,512]{1,0:T(8,128)S(1)} %copy-done.3), kind=kOutput, calls=%fused_computation.17 | convolution fusion | flops 541327360 | bytes 3670024 | tf_op jit(solution)/shard_map/cond/branch_1_fun/dot_general | solution.py:24
  116.1 2.2 %reshape.96 = bf16[512,1,512]{2,1,0:T(2,128)(2,1)S(1)} reshape(bf16[16,2,8192]{2,1,0:T(2,128)(2,1)} %all-to-all-done.1) | data formatting | bytes 1048576
  118.4 3.1 %bitcast_reduce_fusion = bf16[512,512]{1,0:T(8,128)(2,1)S(1)} fusion(bf16[512,1,512]{2,1,0:T(2,128)(2,1)S(1)} %reshape.96), kind=kLoop, calls=%fused_computation.100 | loop fusion | bytes 1048576 | tf_op jit(solution)/shard_map/all_to_all | solution.py:82
  122.0 0.8 copy.49
  (48 shorter events, 8.6 us)
Async XLA Ops:
  0.6 39.0 %copy-start = (bf16[1,1,512,512]{3,2,1,0:T(8,128)(2,1)S(1)}, bf16[1,1,512,512]{3,2,1,0:T(8,128)(2,1)}, u32[]{:S(2)}) copy-start(bf16[1,1,512,512]{3,2,1,0:T(8,128)(2,1)} %param.12) | copy-start | bytes 1572868
  1.8 0.7 copy-start.5
  16.1 23.6 %copy-start.6 = (bf16[1,1,512,512]{3,2,1,0:T(8,128)(2,1)S(1)}, bf16[1,1,512,512]{3,2,1,0:T(8,128)(2,1)}, u32[]{:S(2)}) copy-start(bf16[1,1,512,512]{3,2,1,0:T(8,128)(2,1)} %param.13) | copy-start | bytes 1572868
  16.1 23.6 %all-to-all-start = ((bf16[16,1,32,512]{3,2,1,0:T(8,128)(2,1)}), bf16[16,1,32,512]{3,2,1,0:T(8,128)(2,1)S(1)}, u32[]{:S(2)}, u32[]{:S(2)}) async-start(bf16[16,1,32,512]{3,2,1,0:T(8,128)(2,1)} %constant_dynamic-update-slice_fusion), calls=%async_computation | async-start | bytes 1048576 | tf_op jit(solution)/shard_map/all_to_all | solution.py:53
  47.7 68.4 %all-to-all-start.1 = ((bf16[16,2,8192]{2,1,0:T(2,128)(2,1)}), bf16[16,2,8192]{2,1,0:T(2,128)(2,1)}, u32[]{:S(2)}, u32[]{:S(2)}) async-start(bf16[16,2,8192]{2,1,0:T(2,128)(2,1)} %reshape.95), calls=%async_computation.1 | async-start | bytes 1048576 | tf_op jit(solution)/shard_map/all_to_all | solution.py:82
  96.1 1.5 %copy-start.1 = (f32[1,1,512,512]{3,2,1,0:T(8,128)S(1)}, f32[1,1,512,512]{3,2,1,0:T(8,128)}, u32[]{:S(2)}) copy-start(f32[1,1,512,512]{3,2,1,0:T(8,128)} %param.10) | copy-start | bytes 3145732
  109.8 3.6 %copy-start.2 = (f32[1,1,512,512]{3,2,1,0:T(8,128)S(1)}, f32[1,1,512,512]{3,2,1,0:T(8,128)}, u32[]{:S(2)}) copy-start(f32[1,1,512,512]{3,2,1,0:T(8,128)} %get-tuple-element.60) | copy-start | bytes 3145732 | tf_op jit(solution)/shard_map/cond
  109.8 3.7 %copy-start.3 = (f32[512,512]{1,0:T(8,128)S(1)}, f32[512,512]{1,0:T(8,128)}, u32[]{:S(2)}) copy-start(f32[512,512]{1,0:T(8,128)} %get-tuple-element.58) | copy-start | bytes 3145732 | tf_op jit(solution)/shard_map/cond
  109.8 3.7 %copy-start.4 = (bf16[512,512]{1,0:T(8,128)(2,1)S(1)}, bf16[512,512]{1,0:T(8,128)(2,1)}, u32[]{:S(2)}) copy-start(bf16[512,512]{1,0:T(8,128)(2,1)} %get-tuple-element.91) | copy-start | bytes 1572868 | tf_op jit(solution)/shard_map/cond
